TPU v7x, 512 devices: a whole 4x4x16 slice. The times are simulated.
512 devices in a mesh: tile: 32 (over z, core), chan: 16 (over y, x).
Axes of the slice: x: 4, y: 4, z: 16, core: 2. Of those that a mesh axis runs over, the one named last changes fastest.
Arguments:
- fields: float32 [64, 1024, 411], P('chan', 'tile'), may hold values from -12 to 12
- diffusivity: float32 [64, 1024], P('chan', 'tile'), may hold values from 0.02 to 0.24
- owners: int32 [4096, 1], replicated, may hold values from 0 to 31; in each aligned block of 128 rows (0 to 127, 128 to 255, ...) at most 8 rows name the same one
- observed: bfloat16 [8192, 6144], P('tile', 'chan'), may hold values from -6 to 6
- usable: int32 [8192], P('tile'), may hold values 0 or 1
- w_hidden: bfloat16 [411, 2048], P(None, 'chan'), may hold values from -0.3125 to 0.3125
- b_hidden: float32 [2048], P('chan'), may hold values from -3 to 3
- w_radiance: bfloat16 [2048, 6144], P(None, 'chan'), may hold values from -0.125 to 0.125
- b_radiance: float32 [6144], P('chan'), may hold values from -3 to 3
- inv_cov: bfloat16 [6144, 6144], P('tile', 'chan'), may hold values from -6 to 22
Outputs:
- gradient: float32 [64, 1024, 411], P('chan', 'tile')
Inputs may be any that keep to these rules, and one draw needn't show every extreme that they name: `owners`: in each tile's block of 128 consecutive entries no owner appears more than 8 times, and in some blocks one appears exactly 8 times.
All inputs are finite; a program needn't handle non-finite values. No bound on the sum of `usable` on one device may be relied on, other than what follows from the above.
Results may differ from a plain program's by a relative error of at most 0.0045.
Values may be sent and summed in bfloat16 or wider, within the bound.
A program may use at most 64 MiB of HBM per device.

v0:
```python
import jax
import jax.numpy as jnp
from jax import lax
from jax.sharding import PartitionSpec as P


def padded_2(value, sides, width, wrap):
    for axis, dim in sides:
        devices, length = (lax.axis_size(axis), value.shape[dim])
        up = [(i, (i + 1) % devices) for i in range(devices if wrap else devices - 1)]
        down = [(j, i) for i, j in up]
        last = lax.slice_in_dim(value, length - width, length, axis=dim)
        first = lax.slice_in_dim(value, 0, width, axis=dim)
        before = lax.ppermute(last, axis, up)
        after = lax.ppermute(first, axis, down)
        value = jnp.concatenate([before, value, after], axis=dim)
    return value


def add_rims(values):
    rowwise = padded_2(values, (("chan", 0),), 1, False)
    return padded_2(rowwise, (("tile", 1),), 1, True)


def body(
    fields,
    diffusivity,
    owners,
    observed,
    usable,
    w_hidden,
    b_hidden,
    w_radiance,
    b_radiance,
    inv_cov,
):
    tile_count = lax.axis_size("tile")
    chan_count = lax.axis_size("chan")
    tile_index = lax.axis_index("tile")
    chan_index = lax.axis_index("chan")
    slot_count = observed.shape[0]
    capacity = slot_count // tile_count
    cells_across, cells_along, features = fields.shape
    own_cols = cells_across // 4 * (cells_along // 4)
    tile_cols = chan_count * own_cols
    hidden_dev = w_hidden.shape[1]
    owner_table = owners[:, 0].reshape(tile_count, tile_cols)
    owner_hits = (
        owner_table[:, :, None] == jnp.arange(tile_count, dtype=jnp.int32)[None, None, :]
    ).astype(jnp.int32)
    before = jnp.sum((jnp.cumsum(owner_hits, axis=1) - owner_hits) * owner_hits, axis=2)
    tallies = jnp.sum(owner_hits, axis=1)
    slot_of = lax.dynamic_index_in_dim(
        owner_table * capacity + before, tile_index, 0, keepdims=False
    )
    arriving = lax.dynamic_index_in_dim(tallies, tile_index, 1, keepdims=False)
    occupied = (jnp.arange(capacity, dtype=jnp.int32)[None, :] < arriving[:, None]).reshape(
        slot_count
    )
    grouped = fields.reshape(cells_across // 4, 4, cells_along // 4, 4, features)
    columns = (
        (jnp.sum(grouped, axis=(1, 3)) * 0.0625).reshape(own_cols, features).astype(jnp.bfloat16)
    )
    placer = (slot_of[None, :] == jnp.arange(slot_count, dtype=jnp.int32)[:, None]).astype(
        jnp.bfloat16
    )
    picks = placer
    outgoing = jnp.dot(
        picks,
        lax.all_gather(columns, "chan", axis=0, tiled=True),
        preferred_element_type=jnp.float32,
    )
    incoming = lax.all_to_all(
        outgoing.astype(jnp.bfloat16), "tile", split_axis=0, concat_axis=0, tiled=True
    )
    preact = lax.dot_general(
        w_hidden, incoming, (((0,), (1,)), ((), ())), preferred_element_type=jnp.float32
    )
    preact = preact + b_hidden[:, None]
    squash = jax.nn.sigmoid(preact)
    active = (preact * squash).astype(jnp.bfloat16)
    weights = w_radiance
    radiance = lax.dot_general(
        lax.all_gather(active, "chan", axis=0, tiled=True),
        weights,
        (((0,), (0,)), ((), ())),
        preferred_element_type=jnp.float32,
    )
    radiance = radiance + b_radiance[None, :]
    in_use = usable.astype(jnp.float32) * occupied.astype(jnp.float32)
    departure = ((radiance - observed.astype(jnp.float32)) * in_use[:, None]).astype(jnp.bfloat16)
    all_depart = lax.all_gather(departure, "chan", axis=1, tiled=True)
    picks = all_depart
    cotangent = jnp.dot(
        picks,
        lax.all_gather(inv_cov, "tile", axis=0, tiled=True),
        preferred_element_type=jnp.float32,
    )
    cotangent = cotangent.astype(jnp.bfloat16)
    weights = w_radiance
    full_sum = lax.psum(
        lax.dot_general(
            weights, cotangent, (((1,), (1,)), ((), ())), preferred_element_type=jnp.float32
        ),
        "chan",
    )
    grad_hidden = lax.dynamic_slice_in_dim(full_sum, chan_index * hidden_dev, hidden_dev, 0)
    slope_term = squash * (1.0 + preact * (1.0 - squash))
    grad_pre = (grad_hidden * slope_term).astype(jnp.bfloat16)
    part_grad = lax.dot_general(
        grad_pre, w_hidden, (((0,), (1,)), ((), ())), preferred_element_type=jnp.float32
    )
    summed_grad = lax.psum(part_grad, "chan")
    returned = lax.all_to_all(summed_grad, "tile", split_axis=0, concat_axis=0, tiled=True)
    own_slots = lax.dynamic_slice_in_dim(slot_of, chan_index * own_cols, own_cols, 0)
    column_grad = jnp.take(returned, own_slots, axis=0)
    spread = jnp.repeat(
        column_grad.reshape(cells_across // 4, cells_along // 4, features), 4, axis=0
    )
    adjoint = jnp.repeat(spread, 4, axis=1) * 0.0625
    kappa_root = jnp.sqrt(diffusivity)
    root_rim = add_rims(kappa_root)
    coef_north = (kappa_root * root_rim[2:, 1:-1])[:, :, None]
    coef_south = (kappa_root * root_rim[:-2, 1:-1])[:, :, None]
    coef_east = (kappa_root * root_rim[1:-1, 2:])[:, :, None]
    coef_west = (kappa_root * root_rim[1:-1, :-2])[:, :, None]
    for sweep_index in range(2):
        padded = add_rims(adjoint)
        adjoint = (
            adjoint
            + coef_north * (padded[2:, 1:-1] - adjoint)
            + coef_south * (padded[:-2, 1:-1] - adjoint)
            + coef_east * (padded[1:-1, 2:] - adjoint)
            + coef_west * (padded[1:-1, :-2] - adjoint)
        )
    return adjoint


def solution(mesh):
    placed = (
        P("chan", "tile", None),
        P("chan", "tile"),
        P(),
        P("tile", "chan"),
        P("tile"),
        P(None, "chan"),
        P("chan"),
        P(None, "chan"),
        P("chan"),
        P("tile", "chan"),
    )
    return jax.shard_map(
        body, mesh=mesh, in_specs=placed, out_specs=P("chan", "tile", None), check_vma=False
    )
```

profile of v0, /device:TPU:1, one launch (start us, length us, event | category | flops | bytes accessed | tf_op | source)
XLA Modules:
  0.0 594.1 jit_solution(5220718163068988109)
XLA Ops:
  6.6 0.9 copy.26
  7.5 1.0 reduce_sum.35
  8.6 3.3 convert_reduce_fusion
  12.0 19.6 %all_gather.12 = bf16[128,411]{1,0:T(8,128)(2,1)S(1)} all-gather(bf16[8,411]{1,0:T(8,128)(2,1)S(1)} %multiply_convert_fusion.3), channel_id=1, replica_groups=mesh['tile'=32,'chan'=16] {'chan'}, dimensions={0}, use_global_device_ids=true | all-gather | bytes 111792 | tf_op jit(solution)/shard_map/all_gather | solution.py:70
  32.2 43.2 %all_to_all.24 = bf16[32,8,411]{2,1,0:T(8,128)(2,1)S(1)} all-to-all(bf16[32,8,411]{2,1,0:T(8,128)(2,1)S(1)} %bitcast.26), channel_id=1, replica_groups=mesh['tile'=32,'chan'=16] {'tile'}, dimensions={0} | all-to-all | bytes 420864 | tf_op jit(solution)/shard_map/all_to_all | solution.py:73
  75.4 0.9 multiply_convert_fusion.1
  76.7 45.8 %all-gather.4.cloned.1.call-done = bf16[2048,256]{0,1:T(8,128)(2,1)} async-done(((bf16[128,256]{0,1:T(8,128)(2,1)}), bf16[2048,256]{0,1:T(8,128)(2,1)}) %all-gather.4.cloned.1.call-update) | async-done | bytes 1048592 | tf_op jit(solution)/shard_map/all_gather | solution.py:84
  122.5 2.6 fusion.6
  125.9 66.4 %all-gather.6.cloned.1.call-done = bf16[256,6144]{1,0:T(8,128)(2,1)} async-done(((bf16[256,384]{1,0:T(8,128)(2,1)}), bf16[256,6144]{1,0:T(8,128)(2,1)}) %all-gather.6.cloned.1.call-update) | async-done | bytes 3145744 | tf_op jit(solution)/shard_map/all_gather | solution.py:92
  192.4 77.3 %all-gather.8.cloned.1.call-done = bf16[6144,384]{1,0:T(8,128)(2,1)} async-done(((bf16[192,384]{1,0:T(8,128)(2,1)}), bf16[6144,384]{1,0:T(8,128)(2,1)}) %all-gather.8.cloned.1.call-update) | async-done | bytes 4718608 | tf_op jit(solution)/shard_map/all_gather | solution.py:96
  269.7 7.1 %convolution_bitcast_fusion = f32[2048,256]{0,1:T(8,128)} fusion(bf16[2048,384]{1,0:T(8,128)(2,1)S(1)} %copy-done, bf16[256,6144]{1,0:T(8,128)(2,1)} %all-gather.6.cloned.1.call-done, bf16[6144,384]{1,0:T(8,128)(2,1)} %all-gather.8.cloned.1.call-done), kind=kOutput, calls=%fused_computation.5 | convolution fusion | flops 1610711040 | bytes 11534336 | tf_op jit(solution)/shard_map/dot_general | solution.py:102
  276.9 117.3 %all-reduce.3.cloned.1.call-done = f32[2048,256]{0,1:T(8,128)} async-done(((f32[2048,256]{0,1:T(8,128)}), f32[2048,256]{0,1:T(8,128)}) %all-reduce.3.cloned.1.call-update) | async-done | bytes 2097168 | tf_op jit(solution)/shard_map/psum | solution.py:101
  394.2 2.0 convolution_bitcast_fusion.1
  396.2 116.5 %all-reduce.5.cloned.1.call-done = f32[32,8,411]{2,1,0:T(8,128)} async-done(((f32[32,8,411]{2,1,0:T(8,128)}), f32[32,8,411]{2,1,0:T(8,128)}) %all-reduce.5.cloned.1.call-update) | async-done | bytes 420880 | tf_op jit(solution)/shard_map/psum | solution.py:113
  512.7 15.0 %all-to-all-start.1 = ((f32[32,8,411]{2,1,0:T(8,128)}), f32[32,8,411]{2,1,0:T(8,128)S(1)}, u32[]{:S(2)}, u32[]{:S(2)}) async-start(f32[32,8,411]{2,1,0:T(8,128)} %all-reduce.5.cloned.1.call-done), calls=%async_computation.1 | async-start | bytes 1048576 | tf_op jit(solution)/shard_map/all_to_all | solution.py:114
  527.7 2.8 collective-permute-start.2
  530.5 1.3 collective-permute-start
  532.0 3.1 collective-permute-done
  535.2 1.4 collective-permute-start.4
  536.6 1.4 collective-permute-start.6
  538.0 23.2 %all-to-all-done.1 = f32[32,8,411]{2,1,0:T(8,128)S(1)} async-done(((f32[32,8,411]{2,1,0:T(8,128)}), f32[32,8,411]{2,1,0:T(8,128)S(1)}, u32[]{:S(2)}, u32[]{:S(2)}) %all-to-all-start.1) | async-done | bytes 420896 | tf_op jit(solution)/shard_map/all_to_all | solution.py:114
  561.9 2.8 collective-permute-start.3
  564.7 1.3 collective-permute-start.1
  566.1 3.6 collective-permute-done.1
  569.7 2.2 collective-permute-start.5
  572.0 0.9 collective-permute-done.5
  573.3 2.4 collective-permute-start.9
  575.8 1.3 collective-permute-start.8
  577.1 3.8 collective-permute-done.8
  580.9 4.5 collective-permute-start.10
  585.4 0.8 collective-permute-done.10
  586.6 0.9 fusion.11
  (65 shorter events, 4.0 us)
Async XLA Ops:
  6.5 116.0 %copy-start = (bf16[2048,384]{1,0:T(8,128)(2,1)S(1)}, bf16[2048,384]{1,0:T(8,128)(2,1)}, u32[]{:S(2)}) copy-start(bf16[2048,384]{1,0:T(8,128)(2,1)} %param.17) | copy-start | bytes 4718596
  6.5 68.9 %copy-start.1 = (bf16[411,128]{1,0:T(8,128)(2,1)S(1)}, bf16[411,128]{1,0:T(8,128)(2,1)}, u32[]{:S(2)}) copy-start(bf16[411,128]{1,0:T(8,128)(2,1)} %param.15) | copy-start | bytes 315652
  6.5 68.9 %copy-start.6 = (f32[128]{0:T(128)S(1)}, f32[128]{0:T(128)}, u32[]{:S(2)}) copy-start(f32[128]{0:T(128)} %param.16) | copy-start | bytes 1540
  6.5 70.2 %copy-start.3 = (s32[256]{0:T(256)S(1)}, s32[256]{0:T(256)}, u32[]{:S(2)}) copy-start(s32[256]{0:T(256)} %param.14) | copy-start | bytes 3076
  6.5 116.0 %copy-start.5 = (f32[384]{0:T(512)S(1)}, f32[384]{0:T(512)}, u32[]{:S(2)}) copy-start(f32[384]{0:T(512)} %param.18) | copy-start | bytes 4612
  6.5 115.9 %copy-start.4 = (bf16[256,384]{1,0:T(8,128)(2,1)S(1)}, bf16[256,384]{1,0:T(8,128)(2,1)}, u32[]{:S(2)}) copy-start(bf16[256,384]{1,0:T(8,128)(2,1)} %param.13) | copy-start | bytes 589828
  6.6 115.9 %all-gather.4.cloned.1.call-start = ((), (), s32[]{:S(2)}) async-start(), calls=%async_computation.2 | async-start | bytes 1114112 | tf_op jit(solution)/shard_map/all_gather | solution.py:84
  76.3 116.1 %all-gather.6.cloned.1.call-start = ((), (), s32[]{:S(2)}) async-start(), calls=%async_computation.3 | async-start | bytes 3342336 | tf_op jit(solution)/shard_map/all_gather | solution.py:92
  125.1 144.6 %all-gather.8.cloned.1.call-start = ((), (), s32[]{:S(2)}) async-start(), calls=%async_computation.4 | async-start | bytes 4866048 | tf_op jit(solution)/shard_map/all_gather | solution.py:96
  125.9 268.3 %all-reduce.3.cloned.1.call-start = ((), (), s32[]{:S(2)}) async-start(), calls=%async_computation.5 | async-start | bytes 4194304 | tf_op jit(solution)/shard_map/psum | solution.py:101
  276.8 250.8 %copy-start.2 = (f32[4,32]{1,0:T(4,128)S(1)}, f32[4,32]{1,0:T(4,128)}, u32[]{:S(2)}) copy-start(f32[4,32]{1,0:T(4,128)} %param.11) | copy-start | bytes 1540
  276.8 235.8 %all-reduce.5.cloned.1.call-start = ((), (), s32[]{:S(2)}) async-start(), calls=%async_computation.6 | async-start | bytes 1048576 | tf_op jit(solution)/shard_map/psum | solution.py:113
  512.7 48.5 %all-to-all-start.1 = ((f32[32,8,411]{2,1,0:T(8,128)}), f32[32,8,411]{2,1,0:T(8,128)S(1)}, u32[]{:S(2)}, u32[]{:S(2)}) async-start(f32[32,8,411]{2,1,0:T(8,128)} %all-reduce.5.cloned.1.call-done), calls=%async_computation.1 | async-start | bytes 1048576 | tf_op jit(solution)/shard_map/all_to_all | solution.py:114
  527.7 4.3 collective-permute-start.2
  530.5 4.6 collective-permute-start
  535.2 30.8 %collective-permute-start.4 = (f32[6,1]{1,0:T(8,128)S(1)}, f32[6,1]{1,0:T(8,128)S(1)}, u32[]{:S(2)}, u32[]{:S(2)}) collective-permute-start(f32[6,1]{1,0:T(8,128)S(1)} %get-tuple-element.13), channel_id=1, source_target_pairs={{16,0},{32,16},{48,32},{64,48},{80,64},{96,80},{112,96},{128,112},... | collective-permute-start | bytes 80 | tf_op jit(solution)/shard_map/ppermute | solution.py:15
  536.6 29.4 %collective-permute-start.6 = (f32[6,1]{1,0:T(8,128)S(1)}, f32[6,1]{1,0:T(8,128)S(1)}, u32[]{:S(2)}, u32[]{:S(2)}) collective-permute-start(f32[6,1]{1,0:T(8,128)S(1)} %get-tuple-element.14), channel_id=1, source_target_pairs={{0,16},{16,32},{32,48},{48,64},{64,80},{80,96},{96,112},{112,128},... | collective-permute-start | bytes 80 | tf_op jit(solution)/shard_map/ppermute | solution.py:14
  561.9 4.2 collective-permute-start.3
  564.7 5.0 collective-permute-start.1
  569.7 3.1 collective-permute-start.5
  571.9 1.2 collective-permute-start.7
  573.3 3.8 collective-permute-start.9
  575.8 5.1 collective-permute-start.8
  580.9 5.4 collective-permute-start.10
  585.4 1.2 collective-permute-start.11
Sparse Core Ops, SparseCore 0:
  76.4 46.0 all-gather.3
  125.5 66.8 all-gather.5
  194.5 75.1 all-gather.7
  276.9 117.2 all-reduce.2
  397.2 115.3 all-reduce.4
where the time goes:
time: 600 us; the launch traced here: 594 us
  waiting for transfers between devices  460 us (77%)
  blocking collectives  62.8 us (10%)
  starting transfers between devices  36.6 us (6%)
  between operations  13.4 us (2%)
  matrix products  12.8 us (2%)
    psum x1, waiting for transfers between devices, body(): lax.psum(lax.dot_general(weights, cotangent, (((1,), (1,)), ((), ())), pr...  117 us
    psum x1, waiting for transfers between devices, body(): summed_grad = lax.psum(part_grad, 'chan')  116 us
    all_gather x1, waiting for transfers between devices, body(): lax.all_gather(inv_cov, 'tile', axis=0, tiled=True)  77.3 us
    all_gather x1, waiting for transfers between devices, body(): all_depart = lax.all_gather(departure, 'chan', axis=1, tiled=True)  66.4 us
    all_gather x1, waiting for transfers between devices, body(): lax.all_gather(active, 'chan', axis=0, tiled=True)  45.8 us
    all_to_all x1, blocking collectives, body(): lax.all_to_all(outgoing.astype(jnp.bfloat16), 'tile', split_axis=0, conca...  43.2 us
    all_to_all x1, waiting for transfers between devices, body(): lax.all_to_all(summed_grad, 'tile', split_axis=0, concat_axis=0, tiled=True)  23.2 us
    all_gather x1, blocking collectives, body(): lax.all_gather(columns, 'chan', axis=0, tiled=True)  19.6 us
  transfers between devices with their start and end apart: 18, of which 13 were waited for; matrix products, arithmetic and copies ran while one was open for 0% of the time, Pallas kernels for 0%

commit v1 on v0

v1 whole, which is shorter than its diff:
```python
import jax
import jax.numpy as jnp
from jax import lax
from jax.experimental import pallas as pl
from jax.experimental.pallas import tpu as pltpu
from jax.sharding import PartitionSpec as P

MESH = pl.DeviceIdType.MESH
F32, BF16 = jnp.float32, jnp.bfloat16
NZ, SIDE, NC, NT = 16, 4, 16, 32
CAP = 8
OWN = 8
TC = 128
FEAT, LANES = 411, 512
HID, ALL_HID = 128, 2048
CH = 384
ROWS = 192
HALF = ROWS // 2
UNUSED = 2.0**100

SEMS = (
    "ag1", "ag2", "diff", "obs", "r1a", "r1b", "r2a", "r2b", "core", "a1a", "a1b", "a2a", "a2b", "rs5", "halo",
)


def kernel(
    fields_h, diff_in, owners_in, obs_h, usable_in, wh_h, bh_in, wr_h, br_in, ic_h,
    out,
    fields, quads, obs_send, obs_recv, wh, wr, ic,
    cols, act, gp, r1a, r1b, s1a, s1b, r2a, r2b, g_all, dep, pgrad, rs5, halo, diff, strips, sweep,
    local, send, recv, ring_s, ring_r, hello,
):
    t, c = lax.axis_index("tile"), lax.axis_index("chan")
    z, k = t // 2, t % 2
    y, x = c // SIDE, c % SIDE
    sem_of = {name: i for i, name in enumerate(SEMS)}

    def tile_at(dz, core):
        return lax.rem(z + dz + NZ, NZ) * 2 + core

    def mod(v, n):
        return lax.rem(v + n, n)

    def push(src, dst, name, where):
        i = sem_of[name]
        pltpu.make_async_remote_copy(
            src_ref=src, dst_ref=dst, send_sem=send.at[i], recv_sem=recv.at[i],
            device_id=where, device_id_type=MESH,
        ).start()

    def wait_recv(ref, name):
        pltpu.make_async_copy(ref, ref, recv.at[sem_of[name]]).wait()

    def wait_send(ref, name):
        pltpu.make_async_copy(ref, ref, send.at[sem_of[name]]).wait()

    loads = [
        pltpu.make_async_copy(src, dst, local.at[i])
        for i, (src, dst) in enumerate(
            [(fields_h, fields), (ic_h, ic), (wr_h, wr), (obs_h, obs_send), (wh_h, wh)]
        )
    ]
    for copy in loads:
        copy.start()
    near = [(dz, core) for dz in (4, -4, 3, -3, 2, -2, 1, -1) for core in (0, 1)]
    around = [(dt, dc) for dt in (-1, 0, 1) for dc in (-1, 0, 1) if (dt, dc) != (0, 0)]
    barrier = pltpu.get_barrier_semaphore()
    greeted = [(t, mod(c + i, NC)) for i in range(1, NC)]
    greeted += [(tile_at(dz, core), c) for dz, core in near] + [(z * 2 + 1 - k, c)]
    greeted += [(mod(t + dt, NT), mod(c + dc, NC)) for dt, dc in around if dt and dc]
    for where in greeted:
        pl.semaphore_signal(barrier, inc=1, device_id=where, device_id_type=MESH)

    loads[0].wait()
    summed = fields[0] + fields[1] + fields[2] + fields[3]
    for b in range(LANES // 128):
        width = min(128, FEAT - b * 128)
        quads[b] = jnp.zeros((32, 128), F32)
        quads[b, :, 0:width] = summed[:, b * 128 : b * 128 + width]
        total = None
        for j in range(4):
            part = quads[b, pl.ds(j, OWN, stride=4), :]
            total = part if total is None else total + part
        cols[c, :, b * 128 : b * 128 + 128] = (total * 0.0625).astype(BF16)

    diff[4] = jnp.zeros((8, 128), F32)
    diff[4, 0:4, 0:32] = diff_in[...]

    own_row = jnp.broadcast_to(owners_in[pl.ds(t, 1), :].astype(F32), (TC, TC))
    own_col = jnp.transpose(own_row)
    at_row = lax.broadcasted_iota(jnp.int32, (TC, TC), 0)
    at_lane = lax.broadcasted_iota(jnp.int32, (TC, TC), 1)
    earlier = jnp.where((own_row == own_col) & (at_lane < at_row), 1.0, 0.0)
    rank = jnp.sum(earlier, axis=1, keepdims=True)
    slot = (own_col[:, 0:1] * float(CAP) + rank).astype(jnp.int32)
    select = jnp.where(
        slot == lax.broadcasted_iota(jnp.int32, (TC, NT * CAP), 1), 1.0, 0.0
    ).astype(BF16)

    loads[3].wait()
    usable = usable_in[...].astype(F32)
    usable = jnp.transpose(jnp.concatenate([usable] * 4, axis=0))
    for h in range(2):
        part = slice(h * 16, h * 16 + 16)
        seen = obs_send[part].astype(F32).reshape(TC, CH)
        seen = jnp.where(usable[:, h : h + 1] > 0.5, seen, UNUSED)
        obs_send[part] = seen.reshape(16, CAP, CH).astype(BF16)

    loads[1].wait()
    loads[2].wait()
    cov = ic[...]
    for b in range(NC // 2):
        part = lax.dot_general(
            cov, wr[b * 256 : b * 256 + 256, :], (((1,), (1,)), ((), ())), preferred_element_type=F32
        ).astype(BF16)
        for h in range(2):
            q = 2 * b + h
            gp[q // SIDE, q % SIDE] = part[:, h * 128 : h * 128 + 128]

    pl.semaphore_wait(barrier, len(greeted))

    for i in range(1, NC):
        push(cols.at[c], cols.at[c], "ag1", (t, mod(c + i, NC)))
    for i, (dt, dc) in enumerate(around):
        push(diff.at[4], diff.at[i if i < 4 else i + 1], "diff", (mod(t + dt, NT), mod(c + dc, NC)))
    for step in (SIDE, -SIDE):
        pl.semaphore_signal(hello, inc=1, device_id=(tile_at(step, k), c), device_id_type=MESH)
    own_obs = pltpu.make_async_copy(obs_send.at[t], obs_recv.at[t], local.at[5])
    own_obs.start()

    def send_obs(peers):
        for dz, core in peers:
            to = tile_at(dz, core)
            push(obs_send.at[to], obs_recv.at[t], "obs", (to, c))

    send_obs(near)
    send_obs([(0, 1 - k)])
    for d in range(1, SIDE):
        to_x, to_y = mod(x + d, SIDE), mod(y + d, SIDE)
        push(gp.at[:, to_x, 0:HALF, :], r1a.at[d - 1], "r1a", (t, y * SIDE + to_x))
        push(gp.at[to_y, :, HALF:ROWS, :], r1b.at[d - 1], "r1b", (t, to_y * SIDE + x))
    pl.semaphore_wait(hello, 2)
    send_obs([(dz, core) for dz in (8, 7, -7, 6, -6, 5, -5) for core in (0, 1)])

    loads[4].wait()
    wait_recv(cols.at[0 : NC - 1], "ag1")
    tile_cols = cols[...].astype(F32).reshape(TC, LANES)[:, 0:FEAT].astype(BF16)
    preact = jnp.dot(tile_cols, wh[...], preferred_element_type=F32) + bh_in[...]
    squash = jax.nn.sigmoid(preact)
    act[c] = (preact * squash).astype(BF16)
    slope = squash * (1.0 + preact * (1.0 - squash))
    for i in range(1, NC):
        push(act.at[c], act.at[c], "ag2", (t, mod(c + i, NC)))

    def add(own, got):
        acc = own.astype(F32)
        for d in range(SIDE - 1):
            acc = acc + got[d].astype(F32)
        return acc.astype(BF16)

    wait_recv(r1a, "r1a")
    s1a[...] = add(gp[:, x, 0:HALF, :], r1a)
    wait_recv(r1b, "r1b")
    s1b[...] = add(gp[y, :, HALF:ROWS, :], r1b)
    for d in range(1, SIDE):
        to_x, to_y = mod(x + d, SIDE), mod(y + d, SIDE)
        push(s1a.at[to_y], r2a.at[d - 1], "r2a", (t, to_y * SIDE + x))
        push(s1b.at[to_x], r2b.at[d - 1], "r2b", (t, y * SIDE + to_x))
    wait_recv(r2a, "r2a")
    g_all[z, k, 0:HALF, :] = add(s1a[y], r2a)
    wait_recv(r2b, "r2b")
    g_all[z, k, HALF:ROWS, :] = add(s1b[x], r2b)

    def ring_copy(s, way):
        block = g_all.at[mod(z - s * way, NZ), k]
        i = 0 if way == 1 else 1
        return pltpu.make_async_remote_copy(
            src_ref=block, dst_ref=block, send_sem=ring_s.at[i, s], recv_sem=ring_r.at[i, s],
            device_id=(tile_at(way, k), c), device_id_type=MESH,
        )

    ways = {1: NZ // 2, -1: NZ // 2 - 1}

    def to_core(zz):
        block = g_all.at[zz, k]
        push(block, block, "core", (z * 2 + 1 - k, c))

    def ring_step(s):
        for way, steps in ways.items():
            if 1 <= s <= steps:
                ring_copy(s - 1, way).wait_recv()
            if s < steps:
                ring_copy(s, way).start()
            if 1 <= s <= steps:
                to_core(mod(z - s * way, NZ))

    ring_step(0)
    to_core(z)

    wait_recv(act.at[0 : NC - 1], "ag2")
    tile_act = jnp.concatenate([act[i] for i in range(NC)], axis=1)
    radiance = jnp.dot(tile_act, wr[...], preferred_element_type=F32) + br_in[...]
    own_obs.wait()
    wait_recv(obs_recv.at[0 : NT - 1], "obs")
    arrived = obs_recv[...].astype(F32).reshape(NT * CAP, CH).astype(BF16)
    seen = jnp.dot(select, arrived, preferred_element_type=F32)
    dep[y, x] = jnp.where(seen < UNUSED * 0.5, radiance - seen, 0.0).astype(BF16)
    lo, hi = slice(0, TC // 2), slice(TC // 2, TC)
    for d in range(1, SIDE):
        to_x, to_y = mod(x + d, SIDE), mod(y + d, SIDE)
        push(dep.at[y, x, lo, :], dep.at[y, x, lo, :], "a1a", (t, y * SIDE + to_x))
        push(dep.at[y, x, hi, :], dep.at[y, x, hi, :], "a1b", (t, to_y * SIDE + x))
    ring_step(1)
    ring_step(2)
    wait_recv(dep.at[0, 0:3, lo, :], "a1a")
    for d in range(1, SIDE):
        push(dep.at[y, :, lo, :], dep.at[y, :, lo, :], "a2a", (t, mod(y + d, SIDE) * SIDE + x))
    wait_recv(dep.at[0, 0:3, hi, :], "a1b")
    for d in range(1, SIDE):
        push(dep.at[:, x, hi, :], dep.at[:, x, hi, :], "a2b", (t, y * SIDE + mod(x + d, SIDE)))
    for s in range(3, NZ // 2 + 1):
        ring_step(s)

    wait_recv(diff.at[0:8], "diff")
    lane = lax.broadcasted_iota(jnp.int32, (8, 128), 1)
    row = lax.broadcasted_iota(jnp.int32, (8, 128), 0)
    bands = []
    for dc in range(3):
        west, mid, east = (diff[8 - (dt * 3 + dc)] for dt in range(3))
        bands.append(
            jnp.where(
                lane < 8,
                pltpu.roll(west, 104, 1),
                jnp.where(lane < 40, pltpu.roll(mid, 8, 1), pltpu.roll(east, 40, 1)),
            )
        )
    upper = jnp.where(c > 0, pltpu.roll(bands[0], 6, 0), 0.0)
    lower = jnp.where(c < NC - 1, pltpu.roll(bands[2], 6, 0), 0.0)
    root = jnp.where(row < 2, upper, jnp.where(row < 6, pltpu.roll(bands[1], 2, 0), lower))
    root = jnp.sqrt(jnp.where((lane < 6) | (lane > 41), 0.0, root))
    root = jnp.transpose(root)[0:48, :]
    to_east = root * pltpu.roll(root, 47, 0)
    to_west = root * pltpu.roll(root, 1, 0)

    wait_recv(dep.at[0:3, :, lo, :], "a2a")
    wait_recv(dep.at[0:3, :, hi, :], "a2b")
    wait_recv(g_all.at[:, 0], "core")
    grad = jnp.zeros((TC, HID), F32)
    for b in range(NC):
        grad = grad + jnp.dot(
            dep[b // SIDE, b % SIDE], g_all[b].reshape(2 * ROWS, HID), preferred_element_type=F32
        )
    grad_pre = (grad * slope).astype(BF16)
    part = lax.dot_general(grad_pre, wh[...], (((1,), (1,)), ((), ())), preferred_element_type=F32)
    pgrad[...] = jnp.zeros((NC, OWN, LANES), F32)
    pgrad[:, :, 0:FEAT] = part.reshape(NC, OWN, FEAT)
    for i in range(1, NC):
        to = mod(c + i, NC)
        push(pgrad.at[to], rs5.at[i - 1], "rs5", (t, to))
    wait_recv(rs5, "rs5")
    total = pgrad[c]
    for i in range(NC - 1):
        total = total + rs5[i]
    halo[4] = total * 0.0625
    for i, (dt, dc) in enumerate(around):
        push(halo.at[4], halo.at[i if i < 4 else i + 1], "halo", (mod(t + dt, NT), mod(c + dc, NC)))

    wait_send(cols.at[0 : NC - 1], "ag1")
    wait_send(diff.at[0:8], "diff")
    wait_send(obs_recv.at[0 : NT - 1], "obs")
    wait_send(r1a, "r1a")
    wait_send(r1b, "r1b")
    wait_send(act.at[0 : NC - 1], "ag2")
    wait_send(r2a, "r2a")
    wait_send(r2b, "r2b")
    for way, steps in ways.items():
        for s in range(steps):
            ring_copy(s, way).wait_send()
    wait_send(g_all.at[:, 0], "core")
    wait_send(dep.at[0, 0:3, lo, :], "a1a")
    wait_send(dep.at[0, 0:3, hi, :], "a1b")
    wait_send(dep.at[0:3, :, lo, :], "a2a")
    wait_send(dep.at[0:3, :, hi, :], "a2b")
    wait_send(rs5, "rs5")

    strips[...] = jnp.zeros((3, 48, LANES), F32)
    wait_recv(halo.at[0:8], "halo")
    for dc in range(3):
        west, mid, east = (halo[8 - (dt * 3 + dc)] for dt in range(3))
        strips[dc, 6:8, :] = jnp.broadcast_to(west[7:8, :], (2, LANES))
        strips[dc, 40:42, :] = jnp.broadcast_to(east[0:1, :], (2, LANES))
        for j in range(OWN):
            strips[dc, 8 + 4 * j : 12 + 4 * j, :] = jnp.broadcast_to(mid[j : j + 1, :], (4, LANES))
    wait_send(halo.at[0:8], "halo")

    def swept(mine, before, after, i):
        here = root[:, i : i + 1]
        shape = (48, LANES)
        wide = lambda v: jnp.broadcast_to(v, shape)
        value = mine + wide(here * root[:, i + 1 : i + 2]) * (after - mine)
        value = value + wide(here * root[:, i - 1 : i]) * (before - mine)
        value = value + wide(to_east[:, i : i + 1]) * (pltpu.roll(mine, 47, 0) - mine)
        return value + wide(to_west[:, i : i + 1]) * (pltpu.roll(mine, 1, 0) - mine)

    band = lambda i: strips[0 if i < 2 else (1 if i < 6 else 2)]
    for i in range(1, 7):
        sweep[i - 1] = swept(band(i), band(i - 1), band(i + 1), i)
    for i in range(2, 6):
        out[i - 2] = swept(sweep[i - 1], sweep[i - 2], sweep[i], i)[8:40, 0:FEAT]


def body(fields, diffusivity, owners, observed, usable, w_hidden, b_hidden, w_radiance, b_radiance, inv_cov):
    vmem, hbm = pl.BlockSpec(memory_space=pltpu.VMEM), pl.BlockSpec(memory_space=pl.ANY)
    n = len(SEMS)
    return pl.pallas_call(
        kernel,
        out_shape=jax.ShapeDtypeStruct((4, 32, FEAT), F32),
        in_specs=[hbm, vmem, vmem, hbm, vmem, hbm, vmem, hbm, vmem, hbm],
        out_specs=vmem,
        scratch_shapes=[
            pltpu.VMEM((4, 32, FEAT), F32),
            pltpu.VMEM((4, 32, 128), F32),
            pltpu.VMEM((NT, CAP, CH), BF16),
            pltpu.VMEM((NT, CAP, CH), BF16),
            pltpu.VMEM((FEAT, HID), BF16),
            pltpu.VMEM((ALL_HID, CH), BF16),
            pltpu.VMEM((ROWS, CH), BF16),
            pltpu.VMEM((NC, OWN, LANES), BF16),
            pltpu.VMEM((NC, TC, HID), BF16),
            pltpu.VMEM((SIDE, SIDE, ROWS, HID), BF16),
            pltpu.VMEM((SIDE - 1, SIDE, HALF, HID), BF16),
            pltpu.VMEM((SIDE - 1, SIDE, HALF, HID), BF16),
            pltpu.VMEM((SIDE, HALF, HID), BF16),
            pltpu.VMEM((SIDE, HALF, HID), BF16),
            pltpu.VMEM((SIDE - 1, HALF, HID), BF16),
            pltpu.VMEM((SIDE - 1, HALF, HID), BF16),
            pltpu.VMEM((NZ, 2, ROWS, HID), BF16),
            pltpu.VMEM((SIDE, SIDE, TC, CH), BF16),
            pltpu.VMEM((NC, OWN, LANES), F32),
            pltpu.VMEM((NC - 1, OWN, LANES), F32),
            pltpu.VMEM((9, OWN, LANES), F32),
            pltpu.VMEM((9, 8, 128), F32),
            pltpu.VMEM((3, 48, LANES), F32),
            pltpu.VMEM((6, 48, LANES), F32),
            pltpu.SemaphoreType.DMA((6,)),
            pltpu.SemaphoreType.DMA((n,)),
            pltpu.SemaphoreType.DMA((n,)),
            pltpu.SemaphoreType.DMA((2, NZ // 2)),
            pltpu.SemaphoreType.DMA((2, NZ // 2)),
            pltpu.SemaphoreType.REGULAR,
        ],
        compiler_params=pltpu.CompilerParams(collective_id=0, has_side_effects=True),
    )(
        fields,
        diffusivity,
        owners.reshape(NT, TC),
        observed.reshape(NT, CAP, CH),
        usable.reshape(2, 128),
        w_hidden,
        b_hidden.reshape(1, HID),
        w_radiance,
        b_radiance.reshape(1, CH),
        inv_cov,
    )


def solution(mesh):
    placed = (
        P("chan", "tile", None), P("chan", "tile"), P(), P("tile", "chan"), P("tile"),
        P(None, "chan"), P("chan"), P(None, "chan"), P("chan"), P("tile", "chan"),
    )
    return jax.shard_map(
        body, mesh=mesh, in_specs=placed, out_specs=P("chan", "tile", None), check_vma=False
    )
```

time: 600 us -> 76.5 us (0.13)
  waiting for transfers between devices: 460 us -> 0 us
  Pallas kernels: 0 us -> 73.3 us
  blocking collectives: 62.8 us -> 0 us
  starting transfers between devices: 36.6 us -> 0 us
  between operations: 13.4 us -> 0.01 us
  matrix products: 12.8 us -> 0 us
    psum x2 -> x0, waiting for transfers between devices: 234 us -> none  [the longest x1 117 us: body(): lax.psum(lax.dot_general(weights, cotangent, (((1,), (1,)), ((), ())), pr...]
    all_gather x3 -> x0, waiting for transfers between devices: 190 us -> none  [the longest x1 77.3 us: body(): lax.all_gather(inv_cov, 'tile', axis=0, tiled=True)]
    pallas_call x0 -> x1, Pallas kernels: none -> 73.3 us  [body(): pl.pallas_call(kernel, out_shape=jax.ShapeDtypeStruct((4, 32, FEAT), F32)...]
    all_to_all x1 -> x0, blocking collectives: 43.2 us -> none  [body(): lax.all_to_all(outgoing.astype(jnp.bfloat16), 'tile', split_axis=0, conca...]
    all_to_all x1 -> x0, waiting for transfers between devices: 23.2 us -> none  [body(): lax.all_to_all(summed_grad, 'tile', split_axis=0, concat_axis=0, tiled=True)]
    ppermute x12 -> x0, starting transfers between devices: 21.4 us -> none  [the longest x6 12 us: padded_2(): after = lax.ppermute(first, axis, down)]
    all_gather x1 -> x0, blocking collectives: 19.6 us -> none  [body(): lax.all_gather(columns, 'chan', axis=0, tiled=True)]
    all_to_all x1 -> x0, starting transfers between devices: 15 us -> none  [body(): lax.all_to_all(summed_grad, 'tile', split_axis=0, concat_axis=0, tiled=True)]
  transfers between devices with their start and end apart: 18 -> 0, of which waited for: 13 -> 0; matrix products, arithmetic and copies ran while one was open for 0% -> 0% of each run, Pallas kernels for 0% -> 0%
where the time goes in v1:
time: 76.5 us; the launch traced here: 76.2 us
  Pallas kernels  73.3 us (96%)
  local copies, waits for them, and re-layouts  2.92 us (4%)
    pallas_call x1, Pallas kernels, body(): pl.pallas_call(kernel, out_shape=jax.ShapeDtypeStruct((4, 32, FEAT), F32)...  73.3 us
    unnamed x1, local copies, waits for them, and re-layouts  1.67 us

profile of v1, /device:TPU:1, one launch (start us, length us, event | category | flops | bytes accessed | tf_op | source)
XLA Modules:
  0.0 76.2 jit_solution(3605856547322080979)
XLA Ops:
  0.0 1.2 %reshape.19.br_in = f32[1,384]{1,0:T(1,128)} reshape(f32[384]{0:T(512)} %param.18) | data formatting | bytes 3072 | tf_op jit(solution)/shard_map/reshape | solution.py:362
  1.2 73.3 %shard_map.100 = f32[4,32,411]{2,1,0:T(8,128)} custom-call(f32[4,32,411]{2,1,0:T(8,128)} %fields_h.1, f32[4,32]{1,0:T(4,128)} %diff_in.1, s32[32,128]{1,0:T(8,128)} %bitcast.5, bf16[32,8,384]{2,1,0:T(8,128)(2,1)} %bitcast.4, s32[2,128]{1,0:T(2,128)} %bitcast.6, bf16[411,128]{1,0:T(8,128)(2,1)} %wh_h.1, f32[1,128]{1,0:T(1,128)} %bitcast.7, ...), custom_call_target="tpu_custom_call" | custom-call | tf_op jit(solution)/shard_map/pallas_call | solution.py:315
  74.5 1.7 %copy.12 = f32[4,32,411]{2,1,0:T(8,128)} copy(f32[4,32,411]{2,1,0:T(8,128)} %shard_map.100) | data formatting | bytes 420864

commit v2 on v1

--- a/solution.py
+++ b/solution.py
@@ -19,7 +19,14 @@
 UNUSED = 2.0**100
 
 SEMS = (
-    "ag1", "ag2", "diff", "obs", "r1a", "r1b", "r2a", "r2b", "core", "a1a", "a1b", "a2a", "a2b", "rs5", "halo",
+    "ag1", "ag2", "diff", "obs", "r1a", "r1b", "r2a", "r2b", "a1a", "a1b", "a2a", "a2b", "rs5", "halo",
+)
+
+
+STAGES = (
+    ((0, 3), (0, -3), (0, 1), (0, -1)),
+    ((-3, 3), (3, -3), (-3, 1), (3, -1), (-3, -1), (3, 1)),
+    ((-6, 2), (-6, 1), (6, -1), (-6, -1), (6, 1)),
 )
 
 
@@ -28,7 +35,7 @@
     out,
     fields, quads, obs_send, obs_recv, wh, wr, ic,
     cols, act, gp, r1a, r1b, s1a, s1b, r2a, r2b, g_all, dep, pgrad, rs5, halo, diff, strips, sweep,
-    local, send, recv, ring_s, ring_r, hello,
+    local, send, recv, ring_s, ring_r, core_s, core_r, hello,
 ):
     t, c = lax.axis_index("tile"), lax.axis_index("chan")
     z, k = t // 2, t % 2
@@ -48,11 +55,19 @@
             device_id=where, device_id_type=MESH,
         ).start()
 
-    def wait_recv(ref, name):
-        pltpu.make_async_copy(ref, ref, recv.at[sem_of[name]]).wait()
-
-    def wait_send(ref, name):
-        pltpu.make_async_copy(ref, ref, send.at[sem_of[name]]).wait()
+    lo, hi = slice(0, TC // 2), slice(TC // 2, TC)
+    whole = {
+        "ag1": cols.at[0 : NC - 1], "ag2": act.at[0 : NC - 1], "diff": diff.at[0:8], "obs": obs_recv.at[0 : NT - 1],
+        "r1a": r1a, "r1b": r1b, "r2a": r2a, "r2b": r2b,
+        "a1a": dep.at[0, 0:3, lo, :], "a1b": dep.at[0, 0:3, hi, :],
+        "a2a": dep.at[0:3, :, lo, :], "a2b": dep.at[0:3, :, hi, :], "rs5": rs5, "halo": halo.at[0:8],
+    }
+
+    def wait_recv(name):
+        pltpu.make_async_copy(whole[name], whole[name], recv.at[sem_of[name]]).wait()
+
+    def wait_send(name):
+        pltpu.make_async_copy(whole[name], whole[name], send.at[sem_of[name]]).wait()
 
     loads = [
         pltpu.make_async_copy(src, dst, local.at[i])
@@ -86,6 +101,51 @@
     diff[4] = jnp.zeros((8, 128), F32)
     diff[4, 0:4, 0:32] = diff_in[...]
 
+    pl.semaphore_wait(barrier, len(greeted))
+
+    for i in range(1, NC):
+        push(cols.at[c], cols.at[c], "ag1", (t, mod(c + i, NC)))
+    for i, (dt, dc) in enumerate(around):
+        push(diff.at[4], diff.at[i if i < 4 else i + 1], "diff", (mod(t + dt, NT), mod(c + dc, NC)))
+    for step in (SIDE, -SIDE):
+        pl.semaphore_signal(hello, inc=1, device_id=(tile_at(step, k), c), device_id_type=MESH)
+    loads[3].wait()
+    usable = usable_in[...].astype(F32)
+    usable = jnp.transpose(jnp.concatenate([usable] * 4, axis=0))
+    for h in range(2):
+        part = slice(h * 16, h * 16 + 16)
+        seen = obs_send[part].astype(F32).reshape(TC, CH)
+        seen = jnp.where(usable[:, h : h + 1] > 0.5, seen, UNUSED)
+        obs_send[part] = seen.reshape(16, CAP, CH).astype(BF16)
+
+    own_obs = pltpu.make_async_copy(obs_send.at[t], obs_recv.at[t], local.at[5])
+    own_obs.start()
+
+    def send_obs(peers):
+        for dz, core in peers:
+            to = tile_at(dz, core)
+            push(obs_send.at[to], obs_recv.at[t], "obs", (to, c))
+
+    send_obs(near)
+    send_obs([(0, 1 - k)])
+    loads[1].wait()
+    loads[2].wait()
+    cov = ic[...]
+    for b in range(NC // 2):
+        part = lax.dot_general(
+            cov, wr[b * 256 : b * 256 + 256, :], (((1,), (1,)), ((), ())), preferred_element_type=F32
+        ).astype(BF16)
+        for h in range(2):
+            q = 2 * b + h
+            gp[q // SIDE, q % SIDE] = part[:, h * 128 : h * 128 + 128]
+
+    for d in range(1, SIDE):
+        to_x, to_y = mod(x + d, SIDE), mod(y + d, SIDE)
+        push(gp.at[:, to_x, 0:HALF, :], r1a.at[d - 1], "r1a", (t, y * SIDE + to_x))
+        push(gp.at[to_y, :, HALF:ROWS, :], r1b.at[d - 1], "r1b", (t, to_y * SIDE + x))
+    pl.semaphore_wait(hello, 2)
+    send_obs([(dz, core) for dz in (8, 7, -7, 6, -6, 5, -5) for core in (0, 1)])
+
     own_row = jnp.broadcast_to(owners_in[pl.ds(t, 1), :].astype(F32), (TC, TC))
     own_col = jnp.transpose(own_row)
     at_row = lax.broadcasted_iota(jnp.int32, (TC, TC), 0)
@@ -97,53 +157,8 @@
         slot == lax.broadcasted_iota(jnp.int32, (TC, NT * CAP), 1), 1.0, 0.0
     ).astype(BF16)
 
-    loads[3].wait()
-    usable = usable_in[...].astype(F32)
-    usable = jnp.transpose(jnp.concatenate([usable] * 4, axis=0))
-    for h in range(2):
-        part = slice(h * 16, h * 16 + 16)
-        seen = obs_send[part].astype(F32).reshape(TC, CH)
-        seen = jnp.where(usable[:, h : h + 1] > 0.5, seen, UNUSED)
-        obs_send[part] = seen.reshape(16, CAP, CH).astype(BF16)
-
-    loads[1].wait()
-    loads[2].wait()
-    cov = ic[...]
-    for b in range(NC // 2):
-        part = lax.dot_general(
-            cov, wr[b * 256 : b * 256 + 256, :], (((1,), (1,)), ((), ())), preferred_element_type=F32
-        ).astype(BF16)
-        for h in range(2):
-            q = 2 * b + h
-            gp[q // SIDE, q % SIDE] = part[:, h * 128 : h * 128 + 128]
-
-    pl.semaphore_wait(barrier, len(greeted))
-
-    for i in range(1, NC):
-        push(cols.at[c], cols.at[c], "ag1", (t, mod(c + i, NC)))
-    for i, (dt, dc) in enumerate(around):
-        push(diff.at[4], diff.at[i if i < 4 else i + 1], "diff", (mod(t + dt, NT), mod(c + dc, NC)))
-    for step in (SIDE, -SIDE):
-        pl.semaphore_signal(hello, inc=1, device_id=(tile_at(step, k), c), device_id_type=MESH)
-    own_obs = pltpu.make_async_copy(obs_send.at[t], obs_recv.at[t], local.at[5])
-    own_obs.start()
-
-    def send_obs(peers):
-        for dz, core in peers:
-            to = tile_at(dz, core)
-            push(obs_send.at[to], obs_recv.at[t], "obs", (to, c))
-
-    send_obs(near)
-    send_obs([(0, 1 - k)])
-    for d in range(1, SIDE):
-        to_x, to_y = mod(x + d, SIDE), mod(y + d, SIDE)
-        push(gp.at[:, to_x, 0:HALF, :], r1a.at[d - 1], "r1a", (t, y * SIDE + to_x))
-        push(gp.at[to_y, :, HALF:ROWS, :], r1b.at[d - 1], "r1b", (t, to_y * SIDE + x))
-    pl.semaphore_wait(hello, 2)
-    send_obs([(dz, core) for dz in (8, 7, -7, 6, -6, 5, -5) for core in (0, 1)])
-
     loads[4].wait()
-    wait_recv(cols.at[0 : NC - 1], "ag1")
+    wait_recv("ag1")
     tile_cols = cols[...].astype(F32).reshape(TC, LANES)[:, 0:FEAT].astype(BF16)
     preact = jnp.dot(tile_cols, wh[...], preferred_element_type=F32) + bh_in[...]
     squash = jax.nn.sigmoid(preact)
@@ -158,70 +173,75 @@
             acc = acc + got[d].astype(F32)
         return acc.astype(BF16)
 
-    wait_recv(r1a, "r1a")
+    wait_recv("r1a")
     s1a[...] = add(gp[:, x, 0:HALF, :], r1a)
-    wait_recv(r1b, "r1b")
+    wait_recv("r1b")
     s1b[...] = add(gp[y, :, HALF:ROWS, :], r1b)
     for d in range(1, SIDE):
         to_x, to_y = mod(x + d, SIDE), mod(y + d, SIDE)
         push(s1a.at[to_y], r2a.at[d - 1], "r2a", (t, to_y * SIDE + x))
         push(s1b.at[to_x], r2b.at[d - 1], "r2b", (t, y * SIDE + to_x))
-    wait_recv(r2a, "r2a")
+    def block_of(at, core):
+        return g_all.at[mod(z + at, NZ), core]
+
+    def along(stage, i):
+        at, by = STAGES[stage][i]
+        block = block_of(at, k)
+        return pltpu.make_async_remote_copy(
+            src_ref=block, dst_ref=block, send_sem=ring_s.at[stage, i], recv_sem=ring_r.at[stage, i],
+            device_id=(tile_at(by, k), c), device_id_type=MESH,
+        )
+
+    def across(stage, i, core):
+        at, by = STAGES[stage][i] if stage < 3 else (0, 0)
+        block = block_of(at - by, core)
+        return pltpu.make_async_remote_copy(
+            src_ref=block, dst_ref=block, send_sem=core_s.at[stage, i], recv_sem=core_r.at[stage, i],
+            device_id=(z * 2 + 1 - k, c), device_id_type=MESH,
+        )
+
+    def stage_in(stage):
+        for i in range(len(STAGES[stage])):
+            along(stage, i).wait_recv()
+            if stage < 2:
+                got = STAGES[stage][i][0] - STAGES[stage][i][1]
+                for j, (at, by) in enumerate(STAGES[stage + 1]):
+                    if at == got:
+                        along(stage + 1, j).start()
+        for i in range(len(STAGES[stage])):
+            across(stage, i, k).start()
+
+    wait_recv("r2a")
     g_all[z, k, 0:HALF, :] = add(s1a[y], r2a)
-    wait_recv(r2b, "r2b")
+    wait_recv("r2b")
     g_all[z, k, HALF:ROWS, :] = add(s1b[x], r2b)
-
-    def ring_copy(s, way):
-        block = g_all.at[mod(z - s * way, NZ), k]
-        i = 0 if way == 1 else 1
-        return pltpu.make_async_remote_copy(
-            src_ref=block, dst_ref=block, send_sem=ring_s.at[i, s], recv_sem=ring_r.at[i, s],
-            device_id=(tile_at(way, k), c), device_id_type=MESH,
-        )
-
-    ways = {1: NZ // 2, -1: NZ // 2 - 1}
-
-    def to_core(zz):
-        block = g_all.at[zz, k]
-        push(block, block, "core", (z * 2 + 1 - k, c))
-
-    def ring_step(s):
-        for way, steps in ways.items():
-            if 1 <= s <= steps:
-                ring_copy(s - 1, way).wait_recv()
-            if s < steps:
-                ring_copy(s, way).start()
-            if 1 <= s <= steps:
-                to_core(mod(z - s * way, NZ))
-
-    ring_step(0)
-    to_core(z)
-
-    wait_recv(act.at[0 : NC - 1], "ag2")
+    for i in range(len(STAGES[0])):
+        along(0, i).start()
+    across(3, 0, k).start()
+
+    wait_recv("ag2")
     tile_act = jnp.concatenate([act[i] for i in range(NC)], axis=1)
-    radiance = jnp.dot(tile_act, wr[...], preferred_element_type=F32) + br_in[...]
+    radiance = jnp.dot(tile_act, wr[...], preferred_element_type=F32)
+    radiance = radiance + jnp.concatenate([br_in[i : i + 1, :] for i in range(3)], axis=1)
     own_obs.wait()
-    wait_recv(obs_recv.at[0 : NT - 1], "obs")
+    wait_recv("obs")
     arrived = obs_recv[...].astype(F32).reshape(NT * CAP, CH).astype(BF16)
     seen = jnp.dot(select, arrived, preferred_element_type=F32)
     dep[y, x] = jnp.where(seen < UNUSED * 0.5, radiance - seen, 0.0).astype(BF16)
-    lo, hi = slice(0, TC // 2), slice(TC // 2, TC)
     for d in range(1, SIDE):
         to_x, to_y = mod(x + d, SIDE), mod(y + d, SIDE)
         push(dep.at[y, x, lo, :], dep.at[y, x, lo, :], "a1a", (t, y * SIDE + to_x))
         push(dep.at[y, x, hi, :], dep.at[y, x, hi, :], "a1b", (t, to_y * SIDE + x))
-    ring_step(1)
-    ring_step(2)
-    wait_recv(dep.at[0, 0:3, lo, :], "a1a")
+    stage_in(0)
+    wait_recv("a1a")
     for d in range(1, SIDE):
         push(dep.at[y, :, lo, :], dep.at[y, :, lo, :], "a2a", (t, mod(y + d, SIDE) * SIDE + x))
-    wait_recv(dep.at[0, 0:3, hi, :], "a1b")
+    wait_recv("a1b")
     for d in range(1, SIDE):
         push(dep.at[:, x, hi, :], dep.at[:, x, hi, :], "a2b", (t, y * SIDE + mod(x + d, SIDE)))
-    for s in range(3, NZ // 2 + 1):
-        ring_step(s)
-
-    wait_recv(diff.at[0:8], "diff")
+    stage_in(1)
+
+    wait_recv("diff")
     lane = lax.broadcasted_iota(jnp.int32, (8, 128), 1)
     row = lax.broadcasted_iota(jnp.int32, (8, 128), 0)
     bands = []
@@ -242,14 +262,21 @@
     to_east = root * pltpu.roll(root, 47, 0)
     to_west = root * pltpu.roll(root, 1, 0)
 
-    wait_recv(dep.at[0:3, :, lo, :], "a2a")
-    wait_recv(dep.at[0:3, :, hi, :], "a2b")
-    wait_recv(g_all.at[:, 0], "core")
+    wait_recv("a2a")
+    wait_recv("a2b")
     grad = jnp.zeros((TC, HID), F32)
-    for b in range(NC):
-        grad = grad + jnp.dot(
-            dep[b // SIDE, b % SIDE], g_all[b].reshape(2 * ROWS, HID), preferred_element_type=F32
-        )
+    for stage in (3, 0, 1, 2):
+        entries = STAGES[stage] if stage < 3 else ((0, 0),)
+        if stage == 2:
+            stage_in(2)
+        for i, (at, by) in enumerate(entries):
+            across(stage, i, 1 - k).wait_recv()
+            block = mod(z + at - by, NZ)
+            grad = grad + jnp.dot(
+                dep[block // SIDE, lax.rem(block, SIDE)],
+                g_all[block].reshape(2 * ROWS, HID),
+                preferred_element_type=F32,
+            )
     grad_pre = (grad * slope).astype(BF16)
     part = lax.dot_general(grad_pre, wh[...], (((1,), (1,)), ((), ())), preferred_element_type=F32)
     pgrad[...] = jnp.zeros((NC, OWN, LANES), F32)
@@ -257,7 +284,7 @@
     for i in range(1, NC):
         to = mod(c + i, NC)
         push(pgrad.at[to], rs5.at[i - 1], "rs5", (t, to))
-    wait_recv(rs5, "rs5")
+    wait_recv("rs5")
     total = pgrad[c]
     for i in range(NC - 1):
         total = total + rs5[i]
@@ -265,33 +292,23 @@
     for i, (dt, dc) in enumerate(around):
         push(halo.at[4], halo.at[i if i < 4 else i + 1], "halo", (mod(t + dt, NT), mod(c + dc, NC)))
 
-    wait_send(cols.at[0 : NC - 1], "ag1")
-    wait_send(diff.at[0:8], "diff")
-    wait_send(obs_recv.at[0 : NT - 1], "obs")
-    wait_send(r1a, "r1a")
-    wait_send(r1b, "r1b")
-    wait_send(act.at[0 : NC - 1], "ag2")
-    wait_send(r2a, "r2a")
-    wait_send(r2b, "r2b")
-    for way, steps in ways.items():
-        for s in range(steps):
-            ring_copy(s, way).wait_send()
-    wait_send(g_all.at[:, 0], "core")
-    wait_send(dep.at[0, 0:3, lo, :], "a1a")
-    wait_send(dep.at[0, 0:3, hi, :], "a1b")
-    wait_send(dep.at[0:3, :, lo, :], "a2a")
-    wait_send(dep.at[0:3, :, hi, :], "a2b")
-    wait_send(rs5, "rs5")
+    for name in SEMS[:-1]:
+        wait_send(name)
+    for stage, entries in enumerate(STAGES):
+        for i in range(len(entries)):
+            along(stage, i).wait_send()
+            across(stage, i, k).wait_send()
+    across(3, 0, k).wait_send()
 
     strips[...] = jnp.zeros((3, 48, LANES), F32)
-    wait_recv(halo.at[0:8], "halo")
+    wait_recv("halo")
     for dc in range(3):
         west, mid, east = (halo[8 - (dt * 3 + dc)] for dt in range(3))
         strips[dc, 6:8, :] = jnp.broadcast_to(west[7:8, :], (2, LANES))
         strips[dc, 40:42, :] = jnp.broadcast_to(east[0:1, :], (2, LANES))
         for j in range(OWN):
             strips[dc, 8 + 4 * j : 12 + 4 * j, :] = jnp.broadcast_to(mid[j : j + 1, :], (4, LANES))
-    wait_send(halo.at[0:8], "halo")
+    wait_send("halo")
 
     def swept(mine, before, after, i):
         here = root[:, i : i + 1]
@@ -345,8 +362,10 @@
             pltpu.SemaphoreType.DMA((6,)),
             pltpu.SemaphoreType.DMA((n,)),
             pltpu.SemaphoreType.DMA((n,)),
-            pltpu.SemaphoreType.DMA((2, NZ // 2)),
-            pltpu.SemaphoreType.DMA((2, NZ // 2)),
+            pltpu.SemaphoreType.DMA((3, 6)),
+            pltpu.SemaphoreType.DMA((3, 6)),
+            pltpu.SemaphoreType.DMA((4, 6)),
+            pltpu.SemaphoreType.DMA((4, 6)),
             pltpu.SemaphoreType.REGULAR,
         ],
         compiler_params=pltpu.CompilerParams(collective_id=0, has_side_effects=True),
@@ -359,7 +378,7 @@
         w_hidden,
         b_hidden.reshape(1, HID),
         w_radiance,
-        b_radiance.reshape(1, CH),
+        b_radiance.reshape(3, 128),
         inv_cov,
     )
 

time: 76.5 us -> 67.1 us (0.88)
  Pallas kernels: 73.3 us -> 65.2 us
  local copies, waits for them, and re-layouts: 2.92 us -> 1.67 us
    pallas_call x1, Pallas kernels: 73.3 us -> 65.2 us  [body(): pl.pallas_call(kernel, out_shape=jax.ShapeDtypeStruct((4, 32, FEAT), F32)...]
    reshape x1 -> x0, local copies, waits for them, and re-layouts: 1.24 us -> none  [body(): b_radiance.reshape(1, CH)]
where the time goes in v2:
time: 67.1 us; the launch traced here: 66.9 us
  Pallas kernels  65.2 us (97%)
  local copies, waits for them, and re-layouts  1.67 us (2%)
    pallas_call x1, Pallas kernels, body(): pl.pallas_call(kernel, out_shape=jax.ShapeDtypeStruct((4, 32, FEAT), F32)...  65.2 us
    unnamed x1, local copies, waits for them, and re-layouts  1.67 us

profile of v2, /device:TPU:1, one launch (start us, length us, event | category | flops | bytes accessed | tf_op | source)
XLA Modules:
  0.0 66.9 jit_solution(16173824169396576102)
XLA Ops:
  0.0 65.2 %shard_map.100 = f32[4,32,411]{2,1,0:T(8,128)} custom-call(f32[4,32,411]{2,1,0:T(8,128)} %fields_h.1, f32[4,32]{1,0:T(4,128)} %diff_in.1, s32[32,128]{1,0:T(8,128)} %bitcast.6, bf16[32,8,384]{2,1,0:T(8,128)(2,1)} %bitcast.5, s32[2,128]{1,0:T(2,128)} %bitcast.8, bf16[411,128]{1,0:T(8,128)(2,1)} %wh_h.1, f32[1,128]{1,0:T(1,128)} %bitcast.9, ...), custom_call_target="tpu_custom_call" | custom-call | tf_op jit(solution)/shard_map/pallas_call | solution.py:332
  65.3 1.7 %copy.12 = f32[4,32,411]{2,1,0:T(8,128)} copy(f32[4,32,411]{2,1,0:T(8,128)} %shard_map.100) | data formatting | bytes 420864

commit v3 on v2

--- a/solution.py
+++ b/solution.py
@@ -19,10 +19,9 @@
 UNUSED = 2.0**100
 
 SEMS = (
-    "ag1", "ag2", "diff", "obs", "r1a", "r1b", "r2a", "r2b", "a1a", "a1b", "a2a", "a2b", "rs5", "halo",
+    "ag1", "diff", "obs", "r1a", "r1b", "r2a", "r2b", "rs5", "halo",
+    *(who + part for who in ("act", "dep") for part in ("x1", "x2", "x3", "y1", "y2", "y3", "over_y", "over_x")),
 )
-
-
 STAGES = (
     ((0, 3), (0, -3), (0, 1), (0, -1)),
     ((-3, 3), (3, -3), (-3, 1), (3, -1), (-3, -1), (3, 1)),
@@ -57,17 +56,51 @@
 
     lo, hi = slice(0, TC // 2), slice(TC // 2, TC)
     whole = {
-        "ag1": cols.at[0 : NC - 1], "ag2": act.at[0 : NC - 1], "diff": diff.at[0:8], "obs": obs_recv.at[0 : NT - 1],
-        "r1a": r1a, "r1b": r1b, "r2a": r2a, "r2b": r2b,
-        "a1a": dep.at[0, 0:3, lo, :], "a1b": dep.at[0, 0:3, hi, :],
-        "a2a": dep.at[0:3, :, lo, :], "a2b": dep.at[0:3, :, hi, :], "rs5": rs5, "halo": halo.at[0:8],
+        "ag1": cols.at[0 : NC - 1], "diff": diff.at[0:8], "obs": obs_recv.at[0 : NT - 1],
+        "r1a": r1a, "r1b": r1b, "r2a": r2a, "r2b": r2b, "rs5": rs5, "halo": halo.at[0:8],
     }
+    blocks_of = {"act": act, "dep": dep}
+    for who, buf in blocks_of.items():
+        for d in range(1, SIDE):
+            whole[f"{who}x{d}"] = buf.at[0, 0, lo, :]
+            whole[f"{who}y{d}"] = buf.at[0, 0, hi, :]
+        whole[who + "over_y"] = buf.at[0:3, :, lo, :]
+        whole[who + "over_x"] = buf.at[0:3, :, hi, :]
 
     def wait_recv(name):
         pltpu.make_async_copy(whole[name], whole[name], recv.at[sem_of[name]]).wait()
 
     def wait_send(name):
         pltpu.make_async_copy(whole[name], whole[name], send.at[sem_of[name]]).wait()
+
+    def over_y(who, xx):
+        block = blocks_of[who].at[y, xx, lo, :]
+        for d in (2, 1, 3):
+            push(block, block, who + "over_y", (t, mod(y + d, SIDE) * SIDE + x))
+
+    def over_x(who, yy):
+        block = blocks_of[who].at[yy, x, hi, :]
+        for d in (2, 1, 3):
+            push(block, block, who + "over_x", (t, y * SIDE + mod(x + d, SIDE)))
+
+    def gather(who):
+        upper, lower = blocks_of[who].at[y, x, lo, :], blocks_of[who].at[y, x, hi, :]
+        for d in (2, 1, 3):
+            push(upper, upper, f"{who}x{d}", (t, y * SIDE + mod(x + d, SIDE)))
+            push(lower, lower, f"{who}y{d}", (t, mod(y + d, SIDE) * SIDE + x))
+        over_y(who, x)
+        over_x(who, y)
+
+    def relay(who, *steps):
+        for d in steps:
+            wait_recv(f"{who}x{d}")
+            over_y(who, mod(x - d, SIDE))
+            wait_recv(f"{who}y{d}")
+            over_x(who, mod(y - d, SIDE))
+
+    def gathered(who):
+        wait_recv(who + "over_y")
+        wait_recv(who + "over_x")
 
     loads = [
         pltpu.make_async_copy(src, dst, local.at[i])
@@ -101,6 +134,17 @@
     diff[4] = jnp.zeros((8, 128), F32)
     diff[4, 0:4, 0:32] = diff_in[...]
 
+    loads[1].wait()
+    loads[2].wait()
+    cov = ic[...]
+    for b in range(NC // 2):
+        part = lax.dot_general(
+            cov, wr[b * 256 : b * 256 + 256, :], (((1,), (1,)), ((), ())), preferred_element_type=F32
+        ).astype(BF16)
+        for h in range(2):
+            q = 2 * b + h
+            gp[q // SIDE, q % SIDE] = part[:, h * 128 : h * 128 + 128]
+
     pl.semaphore_wait(barrier, len(greeted))
 
     for i in range(1, NC):
@@ -128,17 +172,6 @@
 
     send_obs(near)
     send_obs([(0, 1 - k)])
-    loads[1].wait()
-    loads[2].wait()
-    cov = ic[...]
-    for b in range(NC // 2):
-        part = lax.dot_general(
-            cov, wr[b * 256 : b * 256 + 256, :], (((1,), (1,)), ((), ())), preferred_element_type=F32
-        ).astype(BF16)
-        for h in range(2):
-            q = 2 * b + h
-            gp[q // SIDE, q % SIDE] = part[:, h * 128 : h * 128 + 128]
-
     for d in range(1, SIDE):
         to_x, to_y = mod(x + d, SIDE), mod(y + d, SIDE)
         push(gp.at[:, to_x, 0:HALF, :], r1a.at[d - 1], "r1a", (t, y * SIDE + to_x))
@@ -162,10 +195,9 @@
     tile_cols = cols[...].astype(F32).reshape(TC, LANES)[:, 0:FEAT].astype(BF16)
     preact = jnp.dot(tile_cols, wh[...], preferred_element_type=F32) + bh_in[...]
     squash = jax.nn.sigmoid(preact)
-    act[c] = (preact * squash).astype(BF16)
+    act[y, x] = (preact * squash).astype(BF16)
     slope = squash * (1.0 + preact * (1.0 - squash))
-    for i in range(1, NC):
-        push(act.at[c], act.at[c], "ag2", (t, mod(c + i, NC)))
+    gather("act")
 
     def add(own, got):
         acc = own.astype(F32)
@@ -208,9 +240,9 @@
                 for j, (at, by) in enumerate(STAGES[stage + 1]):
                     if at == got:
                         along(stage + 1, j).start()
-        for i in range(len(STAGES[stage])):
             across(stage, i, k).start()
 
+    relay("act", 1, 3, 2)
     wait_recv("r2a")
     g_all[z, k, 0:HALF, :] = add(s1a[y], r2a)
     wait_recv("r2b")
@@ -219,8 +251,8 @@
         along(0, i).start()
     across(3, 0, k).start()
 
-    wait_recv("ag2")
-    tile_act = jnp.concatenate([act[i] for i in range(NC)], axis=1)
+    gathered("act")
+    tile_act = jnp.concatenate([act[i // SIDE, i % SIDE] for i in range(NC)], axis=1)
     radiance = jnp.dot(tile_act, wr[...], preferred_element_type=F32)
     radiance = radiance + jnp.concatenate([br_in[i : i + 1, :] for i in range(3)], axis=1)
     own_obs.wait()
@@ -228,17 +260,10 @@
     arrived = obs_recv[...].astype(F32).reshape(NT * CAP, CH).astype(BF16)
     seen = jnp.dot(select, arrived, preferred_element_type=F32)
     dep[y, x] = jnp.where(seen < UNUSED * 0.5, radiance - seen, 0.0).astype(BF16)
-    for d in range(1, SIDE):
-        to_x, to_y = mod(x + d, SIDE), mod(y + d, SIDE)
-        push(dep.at[y, x, lo, :], dep.at[y, x, lo, :], "a1a", (t, y * SIDE + to_x))
-        push(dep.at[y, x, hi, :], dep.at[y, x, hi, :], "a1b", (t, to_y * SIDE + x))
+    gather("dep")
+    relay("dep", 1, 3)
     stage_in(0)
-    wait_recv("a1a")
-    for d in range(1, SIDE):
-        push(dep.at[y, :, lo, :], dep.at[y, :, lo, :], "a2a", (t, mod(y + d, SIDE) * SIDE + x))
-    wait_recv("a1b")
-    for d in range(1, SIDE):
-        push(dep.at[:, x, hi, :], dep.at[:, x, hi, :], "a2b", (t, y * SIDE + mod(x + d, SIDE)))
+    relay("dep", 2)
     stage_in(1)
 
     wait_recv("diff")
@@ -262,8 +287,7 @@
     to_east = root * pltpu.roll(root, 47, 0)
     to_west = root * pltpu.roll(root, 1, 0)
 
-    wait_recv("a2a")
-    wait_recv("a2b")
+    gathered("dep")
     grad = jnp.zeros((TC, HID), F32)
     for stage in (3, 0, 1, 2):
         entries = STAGES[stage] if stage < 3 else ((0, 0),)
@@ -292,8 +316,9 @@
     for i, (dt, dc) in enumerate(around):
         push(halo.at[4], halo.at[i if i < 4 else i + 1], "halo", (mod(t + dt, NT), mod(c + dc, NC)))
 
-    for name in SEMS[:-1]:
-        wait_send(name)
+    for name in SEMS:
+        if name != "halo":
+            wait_send(name)
     for stage, entries in enumerate(STAGES):
         for i in range(len(entries)):
             along(stage, i).wait_send()
@@ -343,7 +368,7 @@
             pltpu.VMEM((ALL_HID, CH), BF16),
             pltpu.VMEM((ROWS, CH), BF16),
             pltpu.VMEM((NC, OWN, LANES), BF16),
-            pltpu.VMEM((NC, TC, HID), BF16),
+            pltpu.VMEM((SIDE, SIDE, TC, HID), BF16),
             pltpu.VMEM((SIDE, SIDE, ROWS, HID), BF16),
             pltpu.VMEM((SIDE - 1, SIDE, HALF, HID), BF16),
             pltpu.VMEM((SIDE - 1, SIDE, HALF, HID), BF16),

time: 67.1 us -> 64.8 us (0.966)
  Pallas kernels: 65.2 us -> 62.9 us
    pallas_call x1, Pallas kernels: 65.2 us -> 62.9 us  [body(): pl.pallas_call(kernel, out_shape=jax.ShapeDtypeStruct((4, 32, FEAT), F32)...]
where the time goes in v3:
time: 64.8 us; the launch traced here: 64.6 us
  Pallas kernels  62.9 us (97%)
  local copies, waits for them, and re-layouts  1.67 us (3%)
    pallas_call x1, Pallas kernels, body(): pl.pallas_call(kernel, out_shape=jax.ShapeDtypeStruct((4, 32, FEAT), F32)...  62.9 us
    unnamed x1, local copies, waits for them, and re-layouts  1.67 us

profile of v3, /device:TPU:1, one launch (start us, length us, event | category | flops | bytes accessed | tf_op | source)
XLA Modules:
  0.0 64.6 jit_solution(14793562145436586903)
XLA Ops:
  0.0 62.9 %shard_map.100 = f32[4,32,411]{2,1,0:T(8,128)} custom-call(f32[4,32,411]{2,1,0:T(8,128)} %fields_h.1, f32[4,32]{1,0:T(4,128)} %diff_in.1, s32[32,128]{1,0:T(8,128)} %bitcast.6, bf16[32,8,384]{2,1,0:T(8,128)(2,1)} %bitcast.5, s32[2,128]{1,0:T(2,128)} %bitcast.8, bf16[411,128]{1,0:T(8,128)(2,1)} %wh_h.1, f32[1,128]{1,0:T(1,128)} %bitcast.9, ...), custom_call_target="tpu_custom_call" | custom-call | tf_op jit(solution)/shard_map/pallas_call | solution.py:357
  62.9 1.7 %copy.12 = f32[4,32,411]{2,1,0:T(8,128)} copy(f32[4,32,411]{2,1,0:T(8,128)} %shard_map.100) | data formatting | bytes 420864

commit v4 on v3

--- a/solution.py
+++ b/solution.py
@@ -232,8 +232,8 @@
             device_id=(z * 2 + 1 - k, c), device_id_type=MESH,
         )
 
-    def stage_in(stage):
-        for i in range(len(STAGES[stage])):
+    def stage_in(stage, only=None):
+        for i in only or range(len(STAGES[stage])):
             along(stage, i).wait_recv()
             if stage < 2:
                 got = STAGES[stage][i][0] - STAGES[stage][i][1]
@@ -261,9 +261,9 @@
     seen = jnp.dot(select, arrived, preferred_element_type=F32)
     dep[y, x] = jnp.where(seen < UNUSED * 0.5, radiance - seen, 0.0).astype(BF16)
     gather("dep")
-    relay("dep", 1, 3)
-    stage_in(0)
-    relay("dep", 2)
+    stage_in(0, (0, 1))
+    relay("dep", 1, 3, 2)
+    stage_in(0, (2, 3))
     stage_in(1)
 
     wait_recv("diff")
@@ -303,15 +303,15 @@
             )
     grad_pre = (grad * slope).astype(BF16)
     part = lax.dot_general(grad_pre, wh[...], (((1,), (1,)), ((), ())), preferred_element_type=F32)
-    pgrad[...] = jnp.zeros((NC, OWN, LANES), F32)
-    pgrad[:, :, 0:FEAT] = part.reshape(NC, OWN, FEAT)
+    part = jnp.concatenate([part, jnp.zeros((TC, LANES - FEAT), F32)], axis=1)
+    pgrad[...] = part.reshape(NC, OWN, LANES).astype(BF16)
     for i in range(1, NC):
         to = mod(c + i, NC)
         push(pgrad.at[to], rs5.at[i - 1], "rs5", (t, to))
     wait_recv("rs5")
-    total = pgrad[c]
+    total = pgrad[c].astype(F32)
     for i in range(NC - 1):
-        total = total + rs5[i]
+        total = total + rs5[i].astype(F32)
     halo[4] = total * 0.0625
     for i, (dt, dc) in enumerate(around):
         push(halo.at[4], halo.at[i if i < 4 else i + 1], "halo", (mod(t + dt, NT), mod(c + dc, NC)))
@@ -378,8 +378,8 @@
             pltpu.VMEM((SIDE - 1, HALF, HID), BF16),
             pltpu.VMEM((NZ, 2, ROWS, HID), BF16),
             pltpu.VMEM((SIDE, SIDE, TC, CH), BF16),
-            pltpu.VMEM((NC, OWN, LANES), F32),
-            pltpu.VMEM((NC - 1, OWN, LANES), F32),
+            pltpu.VMEM((NC, OWN, LANES), BF16),
+            pltpu.VMEM((NC - 1, OWN, LANES), BF16),
             pltpu.VMEM((9, OWN, LANES), F32),
             pltpu.VMEM((9, 8, 128), F32),
             pltpu.VMEM((3, 48, LANES), F32),

time: 64.8 us -> 61.2 us (0.944)
  Pallas kernels: 62.9 us -> 59.3 us
    pallas_call x1, Pallas kernels: 62.9 us -> 59.3 us  [body(): pl.pallas_call(kernel, out_shape=jax.ShapeDtypeStruct((4, 32, FEAT), F32)...]
where the time goes in v4:
time: 61.2 us; the launch traced here: 61 us
  Pallas kernels  59.3 us (97%)
  local copies, waits for them, and re-layouts  1.67 us (3%)
    pallas_call x1, Pallas kernels, body(): pl.pallas_call(kernel, out_shape=jax.ShapeDtypeStruct((4, 32, FEAT), F32)...  59.3 us
    unnamed x1, local copies, waits for them, and re-layouts  1.67 us

profile of v4, /device:TPU:1, one launch (start us, length us, event | category | flops | bytes accessed | tf_op | source)
XLA Modules:
  0.0 61.0 jit_solution(14718340970874146700)
XLA Ops:
  0.0 59.3 %shard_map.100 = f32[4,32,411]{2,1,0:T(8,128)} custom-call(f32[4,32,411]{2,1,0:T(8,128)} %fields_h.1, f32[4,32]{1,0:T(4,128)} %diff_in.1, s32[32,128]{1,0:T(8,128)} %bitcast.6, bf16[32,8,384]{2,1,0:T(8,128)(2,1)} %bitcast.5, s32[2,128]{1,0:T(2,128)} %bitcast.8, bf16[411,128]{1,0:T(8,128)(2,1)} %wh_h.1, f32[1,128]{1,0:T(1,128)} %bitcast.9, ...), custom_call_target="tpu_custom_call" | custom-call | tf_op jit(solution)/shard_map/pallas_call | solution.py:357
  59.3 1.7 %copy.12 = f32[4,32,411]{2,1,0:T(8,128)} copy(f32[4,32,411]{2,1,0:T(8,128)} %shard_map.100) | data formatting | bytes 420864

commit v5 on v4

--- a/solution.py
+++ b/solution.py
@@ -149,6 +149,10 @@
 
     for i in range(1, NC):
         push(cols.at[c], cols.at[c], "ag1", (t, mod(c + i, NC)))
+    for d in range(1, SIDE):
+        to_x, to_y = mod(x + d, SIDE), mod(y + d, SIDE)
+        push(gp.at[:, to_x, 0:HALF, :], r1a.at[d - 1], "r1a", (t, y * SIDE + to_x))
+        push(gp.at[to_y, :, HALF:ROWS, :], r1b.at[d - 1], "r1b", (t, to_y * SIDE + x))
     for i, (dt, dc) in enumerate(around):
         push(diff.at[4], diff.at[i if i < 4 else i + 1], "diff", (mod(t + dt, NT), mod(c + dc, NC)))
     for step in (SIDE, -SIDE):
@@ -172,10 +176,6 @@
 
     send_obs(near)
     send_obs([(0, 1 - k)])
-    for d in range(1, SIDE):
-        to_x, to_y = mod(x + d, SIDE), mod(y + d, SIDE)
-        push(gp.at[:, to_x, 0:HALF, :], r1a.at[d - 1], "r1a", (t, y * SIDE + to_x))
-        push(gp.at[to_y, :, HALF:ROWS, :], r1b.at[d - 1], "r1b", (t, to_y * SIDE + x))
     pl.semaphore_wait(hello, 2)
     send_obs([(dz, core) for dz in (8, 7, -7, 6, -6, 5, -5) for core in (0, 1)])
 

time: 61.2 us -> 61 us (level)
  no operation moved by 1% of the time
where the time goes in v5:
time: 61 us; the launch traced here: 60.7 us
  Pallas kernels  59.1 us (97%)
  local copies, waits for them, and re-layouts  1.67 us (3%)
    pallas_call x1, Pallas kernels, body(): pl.pallas_call(kernel, out_shape=jax.ShapeDtypeStruct((4, 32, FEAT), F32)...  59.1 us
    unnamed x1, local copies, waits for them, and re-layouts  1.67 us

profile of v5, /device:TPU:1, one launch (start us, length us, event | category | flops | bytes accessed | tf_op | source)
XLA Modules:
  0.0 60.7 jit_solution(8695875437444581753)
XLA Ops:
  0.0 59.1 %shard_map.100 = f32[4,32,411]{2,1,0:T(8,128)} custom-call(f32[4,32,411]{2,1,0:T(8,128)} %fields_h.1, f32[4,32]{1,0:T(4,128)} %diff_in.1, s32[32,128]{1,0:T(8,128)} %bitcast.6, bf16[32,8,384]{2,1,0:T(8,128)(2,1)} %bitcast.5, s32[2,128]{1,0:T(2,128)} %bitcast.8, bf16[411,128]{1,0:T(8,128)(2,1)} %wh_h.1, f32[1,128]{1,0:T(1,128)} %bitcast.9, ...), custom_call_target="tpu_custom_call" | custom-call | tf_op jit(solution)/shard_map/pallas_call | solution.py:357
  59.1 1.7 %copy.12 = f32[4,32,411]{2,1,0:T(8,128)} copy(f32[4,32,411]{2,1,0:T(8,128)} %shard_map.100) | data formatting | bytes 420864
